TPU v7x, 256 devices: a whole 4x4x8 slice. The times are simulated.
256 devices in a mesh: gr: 8 (over x, core), gc: 32 (over z, y).
Axes of the slice: x: 4, y: 4, z: 8, core: 2. Of those that a mesh axis runs over, the one named last changes fastest.
Arguments:
- factor_window: bfloat16 [26624, 8192], P('gr', 'gc'), may hold values from -0.0625 to 0.0625
- upper_panel: bfloat16 [8192, 512], P('gc', 'gr'), may hold values from -6 to 6
- panel_block: float32 [26624, 512], P(('gr', 'gc'))
- first_block: int32 [64], P('gc'), may hold values from 0 to 104
Outputs:
- panel_factor: float32 [26624, 512], P(('gr', 'gc'))
All inputs are finite; a program needn't handle non-finite values.
Results may differ from a plain program's by a relative error of at most 0.0003.
Values may be sent and summed in bfloat16 or wider, within the bound.
A program may use at most 64 MiB of HBM per device.

v0:
```python
import jax
import jax.numpy as jnp
from jax import lax
from jax.sharding import PartitionSpec as P

BLK = 128
NS_ITERS = 3


def masked_rows(window_rows, slab_start, col_first):
    row_ids = slab_start + jnp.arange(window_rows.shape[0], dtype=jnp.int32)
    inside = (row_ids // BLK)[:, None] >= col_first[None, :]
    return jnp.where(inside, window_rows, jnp.zeros_like(window_rows))


def body(factor_window, upper_panel, panel_block, first_block):
    row_groups = lax.axis_size("gr")
    col_groups = lax.axis_size("gc")
    local_rows = factor_window.shape[0]
    own_rows = local_rows // col_groups
    panel_width = upper_panel.shape[1] * row_groups
    row_base = lax.axis_index("gr") * local_rows
    col_first = jnp.repeat(first_block, BLK)
    whole_panel = lax.all_gather(upper_panel, "gr", axis=1, tiled=True)
    own_start = lax.axis_index("gc") * own_rows
    summed = lax.psum(
        jnp.dot(
            masked_rows(factor_window, row_base + 0, col_first),
            whole_panel,
            preferred_element_type=jnp.float32,
        ),
        "gc",
    )
    own_update = lax.dynamic_slice_in_dim(summed, own_start, own_rows, 0)
    schur_rows = panel_block - own_update
    global_start = (lax.axis_index("gr") * col_groups + lax.axis_index("gc")) * own_rows
    positions = jnp.arange(panel_width, dtype=jnp.int32) - global_start
    inside = (positions >= 0) & (positions < own_rows)
    picked = jnp.take(schur_rows, jnp.clip(positions, 0, own_rows - 1), axis=0)
    pivot_term = jnp.where(inside[:, None], picked, jnp.zeros_like(picked))
    pivot_block = lax.psum(pivot_term, ("gr", "gc"))
    pivot_scale = jnp.mean(jnp.diagonal(pivot_block))
    scaled = pivot_block / pivot_scale
    inverse = jnp.eye(panel_width, dtype=jnp.float32)
    for iteration in range(NS_ITERS):
        partial_value = jnp.dot(scaled, inverse, precision=lax.Precision.HIGHEST)
        inverse = 2.0 * inverse - jnp.dot(inverse, partial_value, precision=lax.Precision.HIGHEST)
    factor = jnp.dot(schur_rows, inverse, precision=lax.Precision.HIGHEST) / pivot_scale
    rows_global = global_start + jnp.arange(own_rows, dtype=jnp.int32)
    from_inverse = jnp.take(inverse, jnp.clip(rows_global, 0, panel_width - 1), axis=0)
    return jnp.where((rows_global < panel_width)[:, None], from_inverse, factor)


def solution(mesh):
    return jax.shard_map(
        body,
        mesh=mesh,
        in_specs=(P("gr", "gc"), P("gc", "gr"), P(("gr", "gc"), None), P("gc")),
        out_specs=P(("gr", "gc"), None),
        check_vma=False,
    )
```

profile of v0, /device:TPU:1, one launch (start us, length us, event | category | flops | bytes accessed | tf_op | source)
XLA Modules:
  0.0 511.2 jit_solution(6992197898791414502)
XLA Ops:
  6.5 0.0 copy-start
  6.5 0.0 all-reduce.3.cloned.1.call-start
  6.5 16.2 %all_gather.3 = bf16[256,512]{0,1:T(8,128)(2,1)S(1)} all-gather(bf16[256,64]{0,1:T(8,128)(2,1)} %param.5), channel_id=1, replica_groups=mesh['gr'=8,'gc'=32] {'gr'}, dimensions={1}, use_global_device_ids=true | all-gather | bytes 294912 | tf_op jit(solution)/shard_map/all_gather | solution.py:24
  22.7 0.0 copy-done
  22.7 0.1 broadcast_bitcast_fusion
  22.8 5.4 %fusion = f32[3328,512]{1,0:T(8,128)} fusion(bf16[256,512]{0,1:T(8,128)(2,1)S(1)} %all_gather.3, bf16[3328,256]{1,0:T(8,128)(2,1)} %param.4, s32[256]{0:T(256)S(1)} %broadcast_bitcast_fusion, s32[3328]{0:T(1024)S(1)} %add_select_fusion), kind=kOutput, calls=%fused_computation.4 | convolution fusion | flops 874119168 | bytes 8796160 | tf_op jit(solution)/shard_map/dot_general | solution.py:27
  28.2 0.0 copy-start.2
  28.2 0.0 all-reduce.3.cloned.1.call-update
  28.3 0.0 all-reduce.5.cloned.1.call-start
  28.4 191.3 %all-reduce.3.cloned.1.call-done = f32[3328,512]{1,0:T(8,128)} async-done(((f32[3328,512]{1,0:T(8,128)}), f32[3328,512]{1,0:T(8,128)}) %all-reduce.3.cloned.1.call-update) | async-done | bytes 6815760 | tf_op jit(solution)/shard_map/psum | solution.py:26
  219.7 0.0 copy-done.2
  219.7 1.0 dynamic-slice_subtract_fusion
  220.7 1.6 gather_fusion
  222.3 1.2 select_select_fusion
  223.5 0.0 all-reduce.5.cloned.1.call-update
  223.6 258.0 %all-reduce.5.cloned.1.call-done = f32[512,512]{1,0:T(8,128)} async-done(((f32[512,512]{1,0:T(8,128)}), f32[512,512]{1,0:T(8,128)}) %all-reduce.5.cloned.1.call-update) | async-done | bytes 1048592 | tf_op jit(solution)/shard_map/psum | solution.py:41
  481.6 8.6 %gather_fusion.1 = f32[512]{0:T(512)S(1)} fusion(f32[512,512]{1,0:T(8,128)} %all-reduce.5.cloned.1.call-done, s32[512]{0:T(512)S(1)} %bitcast.16), kind=kCustom, calls=%fused_computation.1 | custom fusion | bytes 8192 | tf_op jit(solution)/shard_map/jit(diagonal)/cond/branch_0_fun/gather | solution.py:42
  490.2 0.0 copy-start.1
  490.3 0.6 reduce_sum.9
  491.5 2.2 fusion.4
  493.7 1.1 convolution_subtract_fusion.2
  494.8 0.0 copy-done.1
  494.8 1.9 fusion.16
  496.7 1.9 convolution_subtract_fusion.1
  498.6 1.9 fusion.15
  500.4 1.9 convolution_subtract_fusion
  502.3 0.7 gather_fusion.2
  503.0 1.4 fusion.3
  (8 shorter events, 0.1 us)
Async XLA Ops:
  6.5 16.2 %copy-start = (s32[2]{0:T(128)S(1)}, s32[2]{0:T(128)}, u32[]{:S(2)}) copy-start(s32[2]{0:T(128)} %param.7) | copy-start | bytes 28
  6.5 213.2 %all-reduce.3.cloned.1.call-start = ((), (), s32[]{:S(2)}) async-start(), calls=%async_computation | async-start | bytes 13631488 | tf_op jit(solution)/shard_map/psum | solution.py:26
  28.2 191.5 %copy-start.2 = (f32[104,512]{1,0:T(8,128)S(1)}, f32[104,512]{1,0:T(8,128)}, u32[]{:S(2)}) copy-start(f32[104,512]{1,0:T(8,128)} %param.6) | copy-start | bytes 638980
  28.3 453.4 %all-reduce.5.cloned.1.call-start = ((), (), s32[]{:S(2)}) async-start(), calls=%async_computation.1 | async-start | bytes 2097152 | tf_op jit(solution)/shard_map/psum | solution.py:41
  490.2 4.5 copy-start.1
Sparse Core Ops, SparseCore 0:
  28.4 191.2 all-reduce.2
  225.1 256.4 all-reduce.4
where the time goes:
time: 512 us; the launch traced here: 511 us
  waiting for transfers between devices  449 us (88%)
  matrix products  17.5 us (3%)
  blocking collectives  16.2 us (3%)
  between operations  14.2 us (3%)
  local copies, waits for them, and re-layouts  11 us (2%)
    psum x1, waiting for transfers between devices, body(): pivot_block = lax.psum(pivot_term, ('gr', 'gc'))  258 us
    psum x1, waiting for transfers between devices, body(): lax.psum(jnp.dot(masked_rows(factor_window, row_base + 0, col_first), who...  191 us
    all_gather x1, blocking collectives, body(): whole_panel = lax.all_gather(upper_panel, 'gr', axis=1, tiled=True)  16.2 us
  transfers between devices with their start and end apart: 2, of which 2 were waited for; matrix products, arithmetic and copies ran while one was open for 0% of the time, Pallas kernels for 0%

commit v1 on v0

v1 whole, which is shorter than its diff:
```python
import jax
import jax.numpy as jnp
from jax import lax
from jax.sharding import PartitionSpec as P

BLK = 128
HI = lax.Precision.HIGHEST


def body(factor_window, upper_panel, panel_block, first_block):
    row_groups = lax.axis_size("gr")
    col_groups = lax.axis_size("gc")
    local_rows, local_cols = factor_window.shape
    own_rows = local_rows // col_groups
    width = upper_panel.shape[1] * row_groups
    row_base = lax.axis_index("gr") * local_rows
    col_first = jnp.repeat(first_block, BLK)
    whole_panel = lax.all_gather(upper_panel, "gr", axis=1, tiled=True)
    row_ids = row_base + jnp.arange(local_rows, dtype=jnp.int32)
    masked = jnp.where((row_ids // BLK)[:, None] >= col_first[None, :], factor_window, 0)
    partial = jnp.dot(masked, whole_panel, preferred_element_type=jnp.float32)
    update = lax.psum_scatter(partial, "gc", scatter_dimension=0, tiled=True)
    schur = panel_block - update
    start = (lax.axis_index("gr") * col_groups + lax.axis_index("gc")) * own_rows
    padded = -(-width // own_rows) * own_rows
    spread = jnp.zeros((padded, width), jnp.float32)
    holds = start < width
    at = jnp.where(holds, start, 0)
    spread = lax.dynamic_update_slice(spread, jnp.where(holds, schur, 0.0), (at, 0))[:width]
    piece = lax.psum_scatter(spread, "gc", scatter_dimension=0, tiled=True)
    piece = lax.psum(piece, "gr")
    pivot = lax.all_gather(piece, "gc", axis=0, tiled=True)
    scale = jnp.mean(jnp.diagonal(pivot))
    rows_global = start + jnp.arange(own_rows, dtype=jnp.int32)
    cols = jnp.arange(width, dtype=jnp.int32)
    unit = (rows_global[:, None] == cols[None, :]).astype(jnp.float32)
    left = jnp.where((rows_global < width)[:, None], unit, schur / scale)
    rest = jnp.eye(width, dtype=jnp.float32) - pivot / scale
    square = jnp.dot(rest, rest, precision=HI)
    out = left + jnp.dot(left, rest, precision=HI)
    out = out + jnp.dot(out, square, precision=HI)
    return out + jnp.dot(jnp.dot(out, square, precision=HI), square, precision=HI)


def solution(mesh):
    return jax.shard_map(
        body,
        mesh=mesh,
        in_specs=(P("gr", "gc"), P("gc", "gr"), P(("gr", "gc"), None), P("gc")),
        out_specs=P(("gr", "gc"), None),
        check_vma=False,
    )
```

time: 512 us -> 593 us (1.16)
  waiting for transfers between devices: 449 us -> 509 us
  blocking collectives: 16.2 us -> 43.2 us
  matrix products: 17.5 us -> 10.9 us
    psum x2 -> x0, waiting for transfers between devices: 449 us -> none  [the longest x1 258 us: body(): pivot_block = lax.psum(pivot_term, ('gr', 'gc'))]
    reduce_scatter x0 -> x2, waiting for transfers between devices: none -> 439 us  [the longest x1 224 us: body(): update = lax.psum_scatter(partial, 'gc', scatter_dimension=0, tiled=True)]
    all_gather x0 -> x1, waiting for transfers between devices: none -> 70.1 us  [body(): pivot = lax.all_gather(piece, 'gc', axis=0, tiled=True)]
    psum x0 -> x1, blocking collectives: none -> 27.1 us  [body(): piece = lax.psum(piece, 'gr')]
    dot_general x8 -> x6, matrix products: 17.5 us -> 10.9 us  [the longest x1 5.35 us: body(): partial = jnp.dot(masked, whole_panel, preferred_element_type=jnp.float32)]
  transfers between devices with their start and end apart: 2 -> 3, of which waited for: 2 -> 3; matrix products, arithmetic and copies ran while one was open for 0% -> 0% of each run, Pallas kernels for 0% -> 0%
where the time goes in v1:
time: 593 us; the launch traced here: 589 us
  waiting for transfers between devices  509 us (86%)
  blocking collectives  43.2 us (7%)
  between operations  13.9 us (2%)
  matrix products  10.9 us (2%)
  local copies, waits for them, and re-layouts  9.77 us (2%)
    reduce_scatter x1, waiting for transfers between devices, body(): update = lax.psum_scatter(partial, 'gc', scatter_dimension=0, tiled=True)  224 us
    reduce_scatter x1, waiting for transfers between devices, body(): piece = lax.psum_scatter(spread, 'gc', scatter_dimension=0, tiled=True)  215 us
    all_gather x1, waiting for transfers between devices, body(): pivot = lax.all_gather(piece, 'gc', axis=0, tiled=True)  70.1 us
    psum x1, blocking collectives, body(): piece = lax.psum(piece, 'gr')  27.1 us
    all_gather x1, blocking collectives, body(): whole_panel = lax.all_gather(upper_panel, 'gr', axis=1, tiled=True)  16.1 us
  transfers between devices with their start and end apart: 3, of which 3 were waited for; matrix products, arithmetic and copies ran while one was open for 0% of the time, Pallas kernels for 0%

profile of v1, /device:TPU:1, one launch (start us, length us, event | category | flops | bytes accessed | tf_op | source)
XLA Modules:
  0.0 588.7 jit_solution(15589855183217418392)
XLA Ops:
  6.5 0.0 copy-start
  6.5 0.0 reduce-scatter.3.cloned.1.call-start
  6.6 16.1 %all_gather.6 = bf16[256,512]{0,1:T(8,128)(2,1)S(1)} all-gather(bf16[256,64]{0,1:T(8,128)(2,1)} %param.5), channel_id=1, replica_groups=mesh['gr'=8,'gc'=32] {'gr'}, dimensions={1}, use_global_device_ids=true | all-gather | bytes 294912 | tf_op jit(solution)/shard_map/all_gather | solution.py:18
  22.6 0.0 copy-done
  22.6 0.1 broadcast_bitcast_fusion
  22.7 5.3 fusion
  28.1 0.0 copy-start.2
  28.1 0.0 reduce-scatter.3.cloned.1.call-update
  28.1 0.0 reduce-scatter.5.cloned.1.call-start
  28.2 223.6 %reduce-scatter.3.cloned.1.call-done = f32[104,512]{1,0:T(8,128)} async-done(((f32[3328,512]{1,0:T(8,128)}), f32[104,512]{1,0:T(8,128)}) %reduce-scatter.3.cloned.1.call-update) | async-done | bytes 213008 | tf_op jit(solution)/shard_map/reduce_scatter | solution.py:22
  251.7 0.1 broadcast_in_dim.33
  251.9 0.0 copy-done.2
  251.9 1.0 select_dynamic-update-slice_fusion
  252.9 1.0 slice.6
  253.9 0.0 reduce-scatter.5.cloned.1.call-update
  253.9 0.0 all-gather.2.cloned.1.call-start
  254.0 215.5 %reduce-scatter.5.cloned.1.call-done = f32[16,512]{1,0:T(8,128)} async-done(((f32[512,512]{1,0:T(8,128)}), f32[16,512]{1,0:T(8,128)}) %reduce-scatter.5.cloned.1.call-update) | async-done | bytes 32784 | tf_op jit(solution)/shard_map/reduce_scatter | solution.py:30
  469.5 27.1 %psum.7 = f32[16,512]{1,0:T(8,128)} all-reduce(f32[16,512]{1,0:T(8,128)} %reduce-scatter.5.cloned.1.call-done), channel_id=1, replica_groups=mesh['gr'=8,'gc'=32] {'gr'}, use_global_device_ids=true, to_apply=%region_2.3 | all-reduce | flops 8192 | bytes 65536 | tf_op jit(solution)/shard_map/psum | solution.py:31
  496.6 0.0 all-gather.2.cloned.1.call-update
  496.7 70.1 %all-gather.2.cloned.1.call-done = f32[512,512]{1,0:T(8,128)} async-done(((f32[16,512]{1,0:T(8,128)}), f32[512,512]{1,0:T(8,128)}) %all-gather.2.cloned.1.call-update) | async-done | bytes 1048592 | tf_op jit(solution)/shard_map/all_gather | solution.py:32
  566.8 0.0 copy-start.1
  566.8 8.5 %gather_fusion = f32[512]{0:T(512)S(1)} fusion(f32[512,512]{1,0:T(8,128)} %all-gather.2.cloned.1.call-done, s32[512]{0:T(512)S(1)} %bitcast.10), kind=kCustom, calls=%fused_computation | custom fusion | bytes 8192 | tf_op jit(solution)/shard_map/jit(diagonal)/cond/branch_0_fun/gather | solution.py:33
  575.3 0.6 reduce_sum.9
  576.6 0.0 copy-done.1
  576.6 1.9 fusion.4
  578.5 0.8 convolution_add_fusion.1
  579.4 0.7 convolution_add_fusion
  580.1 0.7 fusion.15
  580.8 1.4 convolution_add_fusion.2
  (4 shorter events, 0.0 us)
Async XLA Ops:
  6.5 16.1 %copy-start = (s32[2]{0:T(128)S(1)}, s32[2]{0:T(128)}, u32[]{:S(2)}) copy-start(s32[2]{0:T(128)} %param.7) | copy-start | bytes 28
  6.5 245.2 %reduce-scatter.3.cloned.1.call-start = ((), (), s32[]{:S(2)}) async-start(), calls=%async_computation.2 | async-start | bytes 7028736 | tf_op jit(solution)/shard_map/reduce_scatter | solution.py:22
  28.1 223.8 %copy-start.2 = (f32[104,512]{1,0:T(8,128)S(1)}, f32[104,512]{1,0:T(8,128)}, u32[]{:S(2)}) copy-start(f32[104,512]{1,0:T(8,128)} %param.6) | copy-start | bytes 638980
  28.1 441.4 %reduce-scatter.5.cloned.1.call-start = ((), (), s32[]{:S(2)}) async-start(), calls=%async_computation.3 | async-start | bytes 1081344 | tf_op jit(solution)/shard_map/reduce_scatter | solution.py:30
  253.9 312.9 %all-gather.2.cloned.1.call-start = ((), (), s32[]{:S(2)}) async-start(), calls=%async_computation.4 | async-start | bytes 1081344 | tf_op jit(solution)/shard_map/all_gather | solution.py:32
  566.8 9.8 %copy-start.1 = (f32[512,512]{1,0:T(8,128)S(1)}, f32[512,512]{1,0:T(8,128)}, u32[]{:S(2)}) copy-start(f32[512,512]{1,0:T(8,128)} %all-gather.2.cloned.1.call-done) | copy-start | bytes 3145732
Sparse Core Ops, SparseCore 0:
  28.2 223.4 reduce-scatter.2
  255.5 213.8 reduce-scatter.4
  496.8 69.9 all-gather.1

commit v2 on v1

v2 whole, which is shorter than its diff:
```python
import jax
import jax.numpy as jnp
from jax import lax
from jax.experimental import pallas as pl
from jax.experimental.pallas import tpu as pltpu
from jax.sharding import PartitionSpec as P

BLK = 128
NX, NC, NY, NZ = 4, 2, 4, 8
PW = 512
ROWS = 104
KC = 256
GW = 64
ROWS_A = 56
POWERS = 7
MESH = pl.DeviceIdType.MESH
F32 = jnp.float32
BF16 = jnp.bfloat16


def split(v):
    hi = v.astype(BF16)
    return hi, (v - hi.astype(F32)).astype(BF16)


def times_transposed(a, bt):
    return lax.dot_general(a, bt, (((1,), (1,)), ((), ())), preferred_element_type=F32)


def kernel(
    window, upper, panel, first, out,
    ut, thr, abuf, mbuf, msend, mrecv, ppan, piece, spread,
    psend, precv, nsend, nrecv,
    loc, uy_s, uy_r, th_s, th_r, ux_s, ux_r, uc_s, uc_r, a_s, a_r, m_s, m_r,
    pan_s, pan_r, mz_s, mz_r, xs_s, xs_r, zs_s, zs_r, ys_s, ys_r, cs_s, cs_r,
    ps_s, ps_r, ns_s, ns_r,
):
    gr, gc = lax.axis_index("gr"), lax.axis_index("gc")
    x, c = gr // NC, gr % NC
    z, y = gc // NY, gc % NY
    pivot_plane = gr == 0
    panel_source = jnp.logical_and(gr == 0, gc < 5)

    def at_y(d):
        return (gr, z * NY + (y + d) % NY)

    def at_z(d):
        return (gr, ((z + d) % NZ) * NY + y)

    def at_x(d):
        return (((x + d) % NX) * NC + c, gc)

    other_core = (x * NC + 1 - c, gc)

    def at_gr(d):
        return ((gr + d) % (NX * NC), gc)

    def remote(src, dst, s, r, who):
        return pltpu.make_async_remote_copy(
            src_ref=src, dst_ref=dst, send_sem=s, recv_sem=r, device_id=who, device_id_type=MESH
        )

    barrier = pltpu.get_barrier_semaphore()
    for d in range(1, NY):
        pl.semaphore_signal(barrier, inc=1, device_id=at_y(d), device_id_type=MESH)
    for d in range(1, NX * NC):
        pl.semaphore_signal(barrier, inc=1, device_id=at_gr(d), device_id_type=MESH)
    for d in range(1, NZ):
        pl.semaphore_signal(barrier, inc=1, device_id=at_z(d), device_id_type=MESH)
    for s in range(2):
        owner = (16 * y + 2 * z + s) // 13

        @pl.when(jnp.logical_and(pivot_plane, owner != gc))
        def _():
            pl.semaphore_signal(barrier, inc=1, device_id=(0, owner), device_id_type=MESH)

    pl.semaphore_wait(barrier, 17 + jnp.where(panel_source, 11 + gc // 4, 0))

    ut[pl.ds(gr * GW, GW), pl.ds(y * KC, KC)] = upper[...]
    lane = lax.broadcasted_iota(jnp.int32, (8, KC), 1)
    thr[:, pl.ds(y * KC, KC)] = jnp.where(lane < BLK, first[0], first[1]) * BLK

    uy = [
        remote(ut.at[pl.ds(gr * GW, GW), pl.ds(y * KC, KC)], ut.at[pl.ds(gr * GW, GW), pl.ds(y * KC, KC)],
               uy_s.at[d - 1], uy_r.at[d - 1], at_y(d))
        for d in range(1, NY)
    ]
    th = [
        remote(thr.at[:, pl.ds(y * KC, KC)], thr.at[:, pl.ds(y * KC, KC)], th_s.at[d - 1], th_r.at[d - 1], at_y(d))
        for d in range(1, NY)
    ]
    for copy in uy + th:
        copy.start()

    mini = [
        remote(window.at[pl.ds(((y + d) % NY) * BLK, BLK), :], mbuf.at[:, pl.ds(y * KC, KC)],
               m_s.at[d - 1], m_r.at[d - 1], at_y(d))
        for d in range(1, NY)
    ]
    mini_own = pltpu.make_async_copy(window.at[pl.ds(y * BLK, BLK), :], mbuf.at[:, pl.ds(y * KC, KC)], loc.at[8])

    @pl.when(pivot_plane)
    def _():
        for copy in mini:
            copy.start()
        mini_own.start()

    order = (4, 3, 5, 2, 6, 1, 7, 0)

    def rows_of(i, yy):
        return pl.ds(pl.multiple_of((((z + order[i]) % NZ) * NY + yy) * ROWS, 8), ROWS)

    exchange, own_rows = [], []
    for i in range(NZ):
        exchange.append([
            remote(window.at[rows_of(i, (y + d) % NY), :], abuf.at[i, :, pl.ds(y * KC, KC)],
                   a_s.at[i, d - 1], a_r.at[i, d - 1], at_y(d))
            for d in range(1, NY)
        ])
        own_rows.append(
            pltpu.make_async_copy(window.at[rows_of(i, y), :], abuf.at[i, :, pl.ds(y * KC, KC)], loc.at[i])
        )
        for copy in exchange[i]:
            copy.start()
        own_rows[i].start()

    def panel_piece(i):
        p = 13 * gc + i
        to = ((p % 16) // 2) * NY + p // 16
        return p, to

    for i in range(13):
        p, to = panel_piece(i)

        @pl.when(jnp.logical_and(jnp.logical_and(panel_source, p < 64), to != gc))
        def _():
            remote(panel.at[pl.ds(8 * i, 8), :], ppan.at[p % 2], pan_s.at[i], pan_r.at[p % 2], (0, to)).start()

        @pl.when(jnp.logical_and(jnp.logical_and(panel_source, p < 64), to == gc))
        def _():
            pltpu.make_async_copy(panel.at[pl.ds(8 * i, 8), :], ppan.at[p % 2], pan_r.at[p % 2]).start()

    def group(d):
        return pl.ds((((x + d) % NX) * NC + c) * GW, GW)

    for copy in uy:
        copy.wait_recv()
    ux = [remote(ut.at[group(0), :], ut.at[group(0), :], ux_s.at[d - 1], ux_r.at[d - 1], at_x(d)) for d in range(1, NX)]
    uc = [remote(ut.at[group(-d), :], ut.at[group(-d), :], uc_s.at[d], uc_r.at[d], other_core) for d in range(NX)]
    for copy in ux:
        copy.start()
    uc[0].start()
    for d in (1, 3, 2):
        ux[d - 1].wait_recv()
        uc[d].start()
    for copy in th:
        copy.wait_recv()
    for copy in uc:
        copy.wait_recv()

    def product(a, row0):
        ids = row0 + lax.broadcasted_iota(jnp.int32, a.shape, 0)
        kept = jnp.where(ids >= thr[0:1, :], a.astype(F32), 0.0).astype(BF16)
        return times_transposed(kept, ut[...])

    mz = [
        remote(msend.at[pl.ds(((z + d) % NZ) * 16, 16), :], mrecv.at[d - 1], mz_s.at[d - 1], mz_r.at[d - 1], at_z(d))
        for d in range(1, NZ)
    ]

    @pl.when(pivot_plane)
    def _():
        mini_own.wait()
        for copy in mini:
            copy.wait_recv()
        msend[...] = product(mbuf[...], y * BLK)
        for copy in mz:
            copy.start()

    def chunk(i):
        own_rows[i].wait()
        for copy in exchange[i]:
            copy.wait_recv()
        return product(abuf[i], gr * (ROWS * NY * NZ) + (((z + order[i]) % NZ) * NY + y) * ROWS)

    parts = (pl.ds(0, ROWS_A), pl.ds(ROWS_A, ROWS - ROWS_A))

    def ring(send, recv, s, r, step):
        return [
            [remote(send.at[k, part, :], recv.at[k, part, :], s.at[k, h], r.at[k, h], at_z(step)) for h, part in enumerate(parts)]
            for k in range(4)
        ]

    plus, minus = ring(psend, precv, ps_s, ps_r, 1), ring(nsend, nrecv, ns_s, ns_r, NZ - 1)

    def first_chunk():
        v = chunk(0)
        psend[0, parts[0], :] = v[:ROWS_A]
        plus[0][0].start()
        nsend[0, parts[1], :] = v[ROWS_A:]
        minus[0][1].start()

    def next_chunk(i, k, ring_, send, recv, came):
        send[k] = chunk(i)
        for h in range(2):
            if h not in came:
                ring_[k][h].start()
        for h in came:
            ring_[k - 1][h].wait_recv()
            send[k, parts[h], :] += recv[k - 1, parts[h], :]
            ring_[k][h].start()

    first_chunk()
    next_chunk(1, 1, plus, psend, precv, (0,))
    next_chunk(2, 1, minus, nsend, nrecv, (1,))

    spread_x = [
        remote(piece.at[(d % NC)], spread.at[y, z, d % NC], xs_s.at[d - 1], xs_r.at[0], (d, gc))
        for d in range(1, NX * NC)
    ]

    @pl.when(pivot_plane)
    def _():
        for copy in mz:
            copy.wait_recv()
        total = msend[pl.ds(z * 16, 16), :]
        for d in range(1, NZ):
            total = total + mrecv[d - 1]
        for s in range(2):
            pltpu.make_async_copy(panel.at[pl.ds(0, 8), :], ppan.at[s], pan_r.at[s]).wait()
            piece[s] = ppan[s] - total[8 * s : 8 * s + 8]
        spread[y, z, 0] = piece[0]
        for copy in spread_x:
            copy.start()

    @pl.when(jnp.logical_not(pivot_plane))
    def _():
        remote(piece.at[0], spread.at[y, z, c], xs_s.at[0], xs_r.at[0], (0, gc)).wait_recv()

    spread_z = [
        remote(spread.at[y, z, c], spread.at[y, z, c], zs_s.at[d - 1], zs_r.at[d - 1], at_z(d)) for d in range(1, NZ)
    ]
    for copy in spread_z:
        copy.start()

    next_chunk(3, 2, plus, psend, precv, (0, 1))
    next_chunk(4, 2, minus, nsend, nrecv, (1, 0))

    for copy in spread_z:
        copy.wait_recv()
    spread_y = [
        remote(spread.at[y, :, c], spread.at[y, :, c], ys_s.at[d - 1], ys_r.at[d - 1], at_y(d)) for d in range(1, NY)
    ]
    spread_c = [
        remote(spread.at[(y + NY - d) % NY, :, c], spread.at[(y + NY - d) % NY, :, c], cs_s.at[d], cs_r.at[d], other_core)
        for d in range(NY)
    ]
    for copy in spread_y:
        copy.start()
    spread_c[0].start()

    next_chunk(5, 3, plus, psend, precv, (0, 1))
    next_chunk(6, 3, minus, nsend, nrecv, (1, 0))
    update = chunk(7)
    for h in range(2):
        plus[3][h].wait_recv()
        minus[3][h].wait_recv()
    schur = panel[...] - (update + precv[3] + nrecv[3])

    for d in (1, 3, 2):
        spread_y[d - 1].wait_recv()
        spread_c[d].start()
    for copy in spread_c:
        copy.wait_recv()

    pivot = spread[...].reshape(PW, PW)
    same = lax.broadcasted_iota(jnp.int32, (PW, PW), 0) == lax.broadcasted_iota(jnp.int32, (PW, PW), 1)
    scale = jnp.sum(jnp.sum(jnp.where(same, pivot, 0.0), axis=0, keepdims=True), axis=1, keepdims=True) / PW
    rest_hi, rest_lo = split(jnp.where(same, 1.0, 0.0) - pivot / scale)
    row_ids = (gr * NY * NZ + gc) * ROWS + lax.broadcasted_iota(jnp.int32, (ROWS, PW), 0)
    unit = jnp.where(row_ids == lax.broadcasted_iota(jnp.int32, (ROWS, PW), 1), 1.0, 0.0)
    left = jnp.where(row_ids < PW, unit, schur / scale)
    total = left
    for _ in range(POWERS):
        hi, lo = split(total)
        total = left + (
            jnp.dot(hi, rest_hi, preferred_element_type=F32)
            + (jnp.dot(hi, rest_lo, preferred_element_type=F32) + jnp.dot(lo, rest_hi, preferred_element_type=F32))
        )
    out[...] = total

    for copy in uy + th + ux + uc + spread_z + spread_y + spread_c:
        copy.wait_send()
    for copies in exchange:
        for copy in copies:
            copy.wait_send()
    plus[0][0].wait_send()
    minus[0][1].wait_send()
    for k in range(1, 4):
        for h in range(2):
            plus[k][h].wait_send()
            minus[k][h].wait_send()

    @pl.when(pivot_plane)
    def _():
        for copy in mini + mz + spread_x:
            copy.wait_send()

    for i in range(13):
        p, to = panel_piece(i)

        @pl.when(jnp.logical_and(jnp.logical_and(panel_source, p < 64), to != gc))
        def _():
            remote(panel.at[pl.ds(8 * i, 8), :], ppan.at[p % 2], pan_s.at[i], pan_r.at[p % 2], (0, to)).wait_send()


def body(window, upper, panel, first):
    vmem, dma = pltpu.VMEM, pltpu.SemaphoreType.DMA
    spec = pl.BlockSpec(memory_space=pltpu.VMEM)

    def both(*shape):
        return [dma(shape), dma(shape)]

    return pl.pallas_call(
        kernel,
        out_shape=jax.ShapeDtypeStruct((ROWS, PW), F32),
        in_specs=[pl.BlockSpec(memory_space=pl.ANY), spec, spec, pl.BlockSpec(memory_space=pltpu.SMEM)],
        out_specs=spec,
        scratch_shapes=[
            vmem((PW, NY * KC), BF16),
            vmem((8, NY * KC), jnp.int32),
            vmem((NZ, ROWS, NY * KC), BF16),
            vmem((BLK, NY * KC), BF16),
            vmem((BLK, PW), F32),
            vmem((NZ - 1, 16, PW), F32),
            vmem((2, 8, PW), F32),
            vmem((2, 8, PW), F32),
            vmem((NY, NZ, NC, 8, PW), F32),
            *[vmem((4, ROWS, PW), F32) for _ in range(4)],
            dma((9,)),
            *both(NY - 1), *both(NY - 1), *both(NX - 1), *both(NX), *both(NZ, NY - 1), *both(NY - 1),
            dma((13,)), dma((2,)), *both(NZ - 1), dma((NX * NC - 1,)), dma((1,)),
            *both(NZ - 1), *both(NY - 1), *both(NY), *both(4, 2), *both(4, 2),
        ],
        compiler_params=pltpu.CompilerParams(
            collective_id=0, has_side_effects=True, vmem_limit_bytes=60 * 1024 * 1024
        ),
        name="panel_update",
    )(window, upper.T, panel, first)


def solution(mesh):
    return jax.shard_map(
        body,
        mesh=mesh,
        in_specs=(P("gr", "gc"), P("gc", "gr"), P(("gr", "gc"), None), P("gc")),
        out_specs=P(("gr", "gc"), None),
        check_vma=False,
    )
```

time: 593 us -> 60.1 us (0.10)
  waiting for transfers between devices: 509 us -> 0 us
  Pallas kernels: 0 us -> 57.6 us
  blocking collectives: 43.2 us -> 0 us
  between operations: 13.9 us -> 0.01 us
  matrix products: 10.9 us -> 0 us
  local copies, waits for them, and re-layouts: 9.77 us -> 1.63 us
    reduce_scatter x2 -> x0, waiting for transfers between devices: 439 us -> none  [the longest x1 224 us: body(): update = lax.psum_scatter(partial, 'gc', scatter_dimension=0, tiled=True)]
    all_gather x1 -> x0, waiting for transfers between devices: 70.1 us -> none  [body(): pivot = lax.all_gather(piece, 'gc', axis=0, tiled=True)]
    pallas_call x0 -> x1, Pallas kernels: none -> 57.6 us  [body(): pl.pallas_call(kernel, out_shape=jax.ShapeDtypeStruct((ROWS, PW), F32), i...]
    psum x1 -> x0, blocking collectives: 27.1 us -> none  [body(): piece = lax.psum(piece, 'gr')]
    all_gather x1 -> x0, blocking collectives: 16.1 us -> none  [body(): whole_panel = lax.all_gather(upper_panel, 'gr', axis=1, tiled=True)]
    dot_general x6 -> x0, matrix products: 10.9 us -> none  [the longest x1 5.35 us: body(): partial = jnp.dot(masked, whole_panel, preferred_element_type=jnp.float32)]
    gather x1 -> x0, local copies, waits for them, and re-layouts: 8.52 us -> none  [body(): scale = jnp.mean(jnp.diagonal(pivot))]
  transfers between devices with their start and end apart: 3 -> 0, of which waited for: 3 -> 0; matrix products, arithmetic and copies ran while one was open for 0% -> 0% of each run, Pallas kernels for 0% -> 0%
where the time goes in v2:
time: 60.1 us; the launch traced here: 59.3 us
  Pallas kernels  57.6 us (96%)
  local copies, waits for them, and re-layouts  1.63 us (3%)
    pallas_call x1, Pallas kernels, body(): pl.pallas_call(kernel, out_shape=jax.ShapeDtypeStruct((ROWS, PW), F32), i...  57.6 us
    unnamed x1, local copies, waits for them, and re-layouts  1.63 us

profile of v2, /device:TPU:1, one launch (start us, length us, event | category | flops | bytes accessed | tf_op | source)
XLA Modules:
  0.0 59.3 jit_solution(1862271247496526955)
XLA Ops:
  0.0 57.6 %panel_update.1 = f32[104,512]{1,0:T(8,128)} custom-call(bf16[3328,256]{1,0:T(8,128)(2,1)} %window.1, bf16[64,256]{1,0:T(8,128)(2,1)} %bitcast.1, f32[104,512]{1,0:T(8,128)} %panel.1, s32[2]{0:T(128)} %first.1), custom_call_target="tpu_custom_call" | custom-call | tf_op jit(solution)/shard_map/panel_update/pallas_call | solution.py:324
  57.6 1.6 %copy.6 = f32[104,512]{1,0:T(8,128)} copy(f32[104,512]{1,0:T(8,128)} %panel_update.1) | data formatting | bytes 425984

commit v3 on v2

v3 whole, which is shorter than its diff:
```python
import jax
import jax.numpy as jnp
from jax import lax
from jax.experimental import pallas as pl
from jax.experimental.pallas import tpu as pltpu
from jax.sharding import PartitionSpec as P

BLK = 128
NX, NC, NY, NZ = 4, 2, 4, 8
PW = 512
ROWS = 104
KC = 256
GW = 64
ROWS_A = 56
POWERS = 7
MESH = pl.DeviceIdType.MESH
F32 = jnp.float32
BF16 = jnp.bfloat16


def split(v):
    hi = v.astype(BF16)
    return hi, (v - hi.astype(F32)).astype(BF16)


def times_transposed(a, bt):
    return lax.dot_general(a, bt, (((1,), (1,)), ((), ())), preferred_element_type=F32)


def kernel(
    window, upper, panel, first, out,
    ut, thr, pown, abuf, mbuf, msend, mrecv, ppan, piece, spread,
    psend, precv, nsend, nrecv,
    loc, sent, uy_r, th_r, ux_r, uc_r, a_r, m_r, pan_r, mz_r, xs_r, zs_r, ys_r, cs_r, ps_r, ns_r,
):
    gr, gc = lax.axis_index("gr"), lax.axis_index("gc")
    x, c = gr // NC, gr % NC
    z, y = gc // NY, gc % NY
    pivot_plane = gr == 0
    panel_source = jnp.logical_and(gr == 0, gc < 5)

    def at_y(d):
        return (gr, z * NY + (y + d) % NY)

    def at_z(d):
        return (gr, ((z + d) % NZ) * NY + y)

    def at_x(d):
        return (((x + d) % NX) * NC + c, gc)

    other_core = (x * NC + 1 - c, gc)

    def at_gr(d):
        return ((gr + d) % (NX * NC), gc)

    def remote(src, dst, s, r, who):
        return pltpu.make_async_remote_copy(
            src_ref=src, dst_ref=dst, send_sem=s, recv_sem=r, device_id=who, device_id_type=MESH
        )

    def arrived(like, sem):
        pltpu.make_async_copy(like, like, sem).wait()

    barrier = pltpu.get_barrier_semaphore()
    for d in range(1, NY):
        pl.semaphore_signal(barrier, inc=1, device_id=at_y(d), device_id_type=MESH)
    for d in range(1, NX * NC):
        pl.semaphore_signal(barrier, inc=1, device_id=at_gr(d), device_id_type=MESH)
    for d in range(1, NZ):
        pl.semaphore_signal(barrier, inc=1, device_id=at_z(d), device_id_type=MESH)
    for s in range(2):
        owner = (16 * y + 2 * z + s) // 13

        @pl.when(jnp.logical_and(pivot_plane, owner != gc))
        def _():
            pl.semaphore_signal(barrier, inc=1, device_id=(0, owner), device_id_type=MESH)

    pl.semaphore_wait(barrier, 17 + jnp.where(panel_source, 11 + gc // 4, 0))

    def group(d):
        return pl.ds((((x + d) % NX) * NC + c) * GW, GW)

    def cols(d):
        return pl.ds(((y + d) % NY) * KC, KC)

    lane = lax.broadcasted_iota(jnp.int32, (8, KC), 1)
    thr[:, pl.ds(y * KC, KC)] = jnp.where(lane < BLK, first[0], first[1]) * BLK
    uy = [remote(upper, ut.at[group(0), cols(0)], sent.at[0], uy_r.at[d - 1], at_y(d)) for d in range(1, NY)]
    th = [
        remote(thr.at[:, cols(0)], thr.at[:, cols(0)], sent.at[1], th_r, at_y(d)) for d in range(1, NY)
    ]
    ux = [
        [
            remote(ut.at[group(0), cols(-j)] if j else upper, ut.at[group(0), cols(-j)],
                   sent.at[2], ux_r.at[d - 1], at_x(d))
            for j in range(NY)
        ]
        for d in range(1, NX)
    ]
    upper_own = pltpu.make_async_copy(upper, ut.at[group(0), cols(0)], loc.at[0])
    panel_own = pltpu.make_async_copy(panel, pown, loc.at[1])
    for d in (1, 3, 2):
        uy[d - 1].start()
    for d in (1, 3, 2):
        ux[d - 1][0].start()
    for copy in th:
        copy.start()
    upper_own.start()

    mini = [
        remote(window.at[pl.ds(((y + d) % NY) * BLK, BLK), :], mbuf.at[:, pl.ds(y * KC, KC)],
               sent.at[4], m_r, at_y(d))
        for d in range(1, NY)
    ]
    mini_own = pltpu.make_async_copy(window.at[pl.ds(y * BLK, BLK), :], mbuf.at[:, pl.ds(y * KC, KC)], m_r)

    @pl.when(pivot_plane)
    def _():
        for copy in mini:
            copy.start()
        mini_own.start()

    order = (4, 3, 5, 2, 6, 1, 7, 0)

    def rows_of(i, yy):
        return pl.ds(pl.multiple_of((((z + order[i]) % NZ) * NY + yy) * ROWS, 8), ROWS)

    exchange, own_rows = [], []
    for i in range(NZ):
        exchange.append([
            remote(window.at[rows_of(i, (y + d) % NY), :], abuf.at[i, :, pl.ds(y * KC, KC)],
                   sent.at[5], a_r.at[i], at_y(d))
            for d in range(1, NY)
        ])
        own_rows.append(
            pltpu.make_async_copy(window.at[rows_of(i, y), :], abuf.at[i, :, pl.ds(y * KC, KC)], a_r.at[i])
        )
        for copy in exchange[i]:
            copy.start()
        own_rows[i].start()

    panel_own.start()

    def panel_piece(i):
        p = 13 * gc + i
        to = ((p % 16) // 2) * NY + p // 16
        return p, to

    for i in range(13):
        p, to = panel_piece(i)

        @pl.when(jnp.logical_and(jnp.logical_and(panel_source, p < 64), to != gc))
        def _():
            remote(panel.at[pl.ds(8 * i, 8), :], ppan.at[p % 2], sent.at[6], pan_r, (0, to)).start()

        @pl.when(jnp.logical_and(jnp.logical_and(panel_source, p < 64), to == gc))
        def _():
            pltpu.make_async_copy(panel.at[pl.ds(8 * i, 8), :], ppan.at[p % 2], pan_r).start()

    for j in (1, 3, 2):
        uy[j - 1].wait_recv()
        for d in (1, 3, 2):
            ux[d - 1][j].start()
    uc = [remote(ut.at[group(-d), :], ut.at[group(-d), :], sent.at[3], uc_r, other_core) for d in range(NX)]
    upper_own.wait()
    uc[0].start()
    for d in (1, 3, 2):
        arrived(ut.at[group(-d), :], ux_r.at[d - 1])
        uc[d].start()
    arrived(thr.at[:, pl.ds(0, (NY - 1) * KC)], th_r)
    arrived(ut.at[pl.ds(0, PW // NC), :], uc_r)

    def product(a, row0):
        ids = row0 + lax.broadcasted_iota(jnp.int32, a.shape, 0)
        kept = jnp.where(ids >= thr[0:1, :], a.astype(F32), 0.0).astype(BF16)
        return times_transposed(kept, ut[...])

    mz = [
        remote(msend.at[pl.ds(((z + d) % NZ) * 16, 16), :], mrecv.at[d - 1], sent.at[7], mz_r, at_z(d))
        for d in range(1, NZ)
    ]

    @pl.when(pivot_plane)
    def _():
        arrived(mbuf, m_r)
        msend[...] = product(mbuf[...], y * BLK)
        for copy in mz:
            copy.start()

    def chunk(i):
        arrived(abuf.at[i], a_r.at[i])
        return product(abuf[i], gr * (ROWS * NY * NZ) + (((z + order[i]) % NZ) * NY + y) * ROWS)

    parts = (pl.ds(0, ROWS_A), pl.ds(ROWS_A, ROWS - ROWS_A))

    def ring(send, recv, r, step):
        return [
            [remote(send.at[k, part, :], recv.at[k, part, :], sent.at[8], r.at[k, h], at_z(step)) for h, part in enumerate(parts)]
            for k in range(4)
        ]

    plus, minus = ring(psend, precv, ps_r, 1), ring(nsend, nrecv, ns_r, NZ - 1)

    def forward(k, h):
        plus[k - 1][h].wait_recv()
        psend[k, parts[h], :] += precv[k - 1, parts[h], :]
        plus[k][h].start()
        minus[k - 1][1 - h].wait_recv()
        nsend[k, parts[1 - h], :] += nrecv[k - 1, parts[1 - h], :]
        minus[k][1 - h].start()

    update = chunk(0)
    psend[0, parts[0], :] = update[:ROWS_A]
    plus[0][0].start()
    nsend[0, parts[1], :] = update[ROWS_A:]
    minus[0][1].start()
    psend[1] = chunk(1)
    plus[1][1].start()
    spread_x = [
        remote(piece.at[(d % NC)], spread.at[y, z, d % NC], sent.at[9], xs_r, (d, gc))
        for d in range(1, NX * NC)
    ]

    spread_z = [
        remote(spread.at[y, z, c], spread.at[y, z, c], sent.at[10], zs_r.at[d - 1], at_z(d)) for d in range(1, NZ)
    ]
    spread_y = [
        [
            remote(spread.at[y, (z + NZ - j) % NZ, c], spread.at[y, (z + NZ - j) % NZ, c],
                   sent.at[11], ys_r.at[d - 1], at_y(d))
            for j in range(NZ)
        ]
        for d in range(1, NY)
    ]

    def spread_own():
        for d in (4, 3, 5, 2, 6, 1, 7):
            spread_z[d - 1].start()
        for d in (1, 3, 2):
            spread_y[d - 1][0].start()

    @pl.when(pivot_plane)
    def _():
        arrived(mrecv, mz_r)
        arrived(ppan, pan_r)
        total = msend[pl.ds(z * 16, 16), :]
        for d in range(1, NZ):
            total = total + mrecv[d - 1]
        for s in range(2):
            piece[s] = ppan[s] - total[8 * s : 8 * s + 8]
        spread[y, z, 0] = piece[0]
        for copy in spread_x:
            copy.start()
        spread_own()

    nsend[1] = chunk(2)
    minus[1][0].start()
    forward(1, 0)
    psend[2] = chunk(3)
    nsend[2] = chunk(4)
    forward(2, 1)

    forward(2, 0)

    @pl.when(jnp.logical_not(pivot_plane))
    def _():
        remote(piece.at[0], spread.at[y, z, c], sent.at[9], xs_r, (0, gc)).wait_recv()
        spread_own()


    psend[3] = chunk(5)
    nsend[3] = chunk(6)
    forward(3, 1)
    forward(3, 0)

    for j in (1, 7, 2, 6, 3, 5, 4):
        spread_z[j - 1].wait_recv()
        for d in (1, 3, 2):
            spread_y[d - 1][j].start()
    spread_c = [
        remote(spread.at[(y + NY - d) % NY, :, c], spread.at[(y + NY - d) % NY, :, c], sent.at[12], cs_r, other_core)
        for d in range(NY)
    ]
    spread_c[0].start()

    update = chunk(7)
    panel_own.wait()
    for h in (1, 0):
        plus[3][h].wait_recv()
        minus[3][1 - h].wait_recv()
    schur = pown[...] - (update + precv[3] + nrecv[3])

    for d in (1, 3, 2):
        arrived(spread.at[0, :, 0], ys_r.at[d - 1])
        spread_c[d].start()
    arrived(spread.at[:, :, 0], cs_r)

    pivot = spread[...].reshape(PW, PW)
    same = lax.broadcasted_iota(jnp.int32, (PW, PW), 0) == lax.broadcasted_iota(jnp.int32, (PW, PW), 1)
    scale = jnp.sum(jnp.sum(jnp.where(same, pivot, 0.0), axis=0, keepdims=True), axis=1, keepdims=True) / PW
    rest_hi, rest_lo = split(jnp.where(same, 1.0, 0.0) - pivot / scale)
    row_ids = (gr * NY * NZ + gc) * ROWS + lax.broadcasted_iota(jnp.int32, (ROWS, PW), 0)
    unit = jnp.where(row_ids == lax.broadcasted_iota(jnp.int32, (ROWS, PW), 1), 1.0, 0.0)
    left = jnp.where(row_ids < PW, unit, schur / scale)
    total = left
    for _ in range(POWERS):
        hi, lo = split(total)
        both = jnp.dot(jnp.concatenate([hi, lo]), rest_hi, preferred_element_type=F32)
        total = left + (both[:ROWS] + (both[ROWS:] + jnp.dot(hi, rest_lo, preferred_element_type=F32)))
    out[...] = total

    arrived(ut.at[pl.ds(0, 48), :], sent.at[0])
    arrived(thr.at[:, pl.ds(0, (NY - 1) * KC)], sent.at[1])
    arrived(ut.at[pl.ds(0, 3 * GW), :], sent.at[2])
    arrived(ut.at[pl.ds(0, PW // NC), :], sent.at[3])
    arrived(abuf.at[:, :, pl.ds(0, (NY - 1) * KC)], sent.at[5])
    arrived(abuf.at[:, :, pl.ds(0, 7 * BLK)], sent.at[8])
    arrived(spread.at[0, pl.ds(0, NZ - 1), 0], sent.at[10])
    arrived(spread.at[pl.ds(0, NY - 1), :, 0], sent.at[11])
    arrived(spread.at[:, :, 0], sent.at[12])

    @pl.when(pivot_plane)
    def _():
        arrived(mbuf.at[:, pl.ds(0, (NY - 1) * KC)], sent.at[4])
        arrived(mrecv, sent.at[7])
        arrived(spread.at[0, pl.ds(0, NZ - 1), 0], sent.at[9])

    @pl.when(jnp.logical_and(gr == 0, gc < 4))
    def _():
        arrived(panel.at[pl.ds(0, 88), :], sent.at[6])

    @pl.when(jnp.logical_and(gr == 0, gc == 4))
    def _():
        arrived(panel.at[pl.ds(0, 96), :], sent.at[6])


def body(window, upper, panel, first):
    vmem, dma = pltpu.VMEM, pltpu.SemaphoreType.DMA
    spec = pl.BlockSpec(memory_space=pltpu.VMEM)

    return pl.pallas_call(
        kernel,
        out_shape=jax.ShapeDtypeStruct((ROWS, PW), F32),
        in_specs=[*[pl.BlockSpec(memory_space=pl.ANY)] * 3, pl.BlockSpec(memory_space=pltpu.SMEM)],
        out_specs=spec,
        scratch_shapes=[
            vmem((PW, NY * KC), BF16),
            vmem((8, NY * KC), jnp.int32),
            vmem((ROWS, PW), F32),
            vmem((NZ, ROWS, NY * KC), BF16),
            vmem((BLK, NY * KC), BF16),
            vmem((BLK, PW), F32),
            vmem((NZ - 1, 16, PW), F32),
            vmem((2, 8, PW), F32),
            vmem((2, 8, PW), F32),
            vmem((NY, NZ, NC, 8, PW), F32),
            *[vmem((4, ROWS, PW), F32) for _ in range(4)],
            dma((2,)), dma((13,)),
            dma((NY - 1,)), dma, dma((NX - 1,)), dma, dma((NZ,)), dma, dma, dma, dma,
            dma((NZ - 1,)), dma((NY - 1,)), dma, dma((4, 2)), dma((4, 2)),
        ],
        compiler_params=pltpu.CompilerParams(
            collective_id=0, has_side_effects=True, vmem_limit_bytes=63 * 1024 * 1024
        ),
        name="panel_update",
    )(window, upper.T, panel, first)


def solution(mesh):
    return jax.shard_map(
        body,
        mesh=mesh,
        in_specs=(P("gr", "gc"), P("gc", "gr"), P(("gr", "gc"), None), P("gc")),
        out_specs=P(("gr", "gc"), None),
        check_vma=False,
    )
```

time: 60.1 us -> 55.3 us (0.920); the launches traced: 59.3 us -> 55.2 us
  Pallas kernels: 57.6 us -> 53.6 us
    pallas_call x1, Pallas kernels: 57.6 us -> 53.6 us  [body(): pl.pallas_call(kernel, out_shape=jax.ShapeDtypeStruct((ROWS, PW), F32), i...]
where the time goes in v3:
time: 55.3 us; the launch traced here: 55.2 us
  Pallas kernels  53.6 us (97%)
  local copies, waits for them, and re-layouts  1.63 us (3%)
    pallas_call x1, Pallas kernels, body(): pl.pallas_call(kernel, out_shape=jax.ShapeDtypeStruct((ROWS, PW), F32), i...  53.6 us
    unnamed x1, local copies, waits for them, and re-layouts  1.63 us

profile of v3, /device:TPU:1, one launch (start us, length us, event | category | flops | bytes accessed | tf_op | source)
XLA Modules:
  0.0 55.2 jit_solution(579936018073780351)
XLA Ops:
  0.0 53.6 %panel_update.1 = f32[104,512]{1,0:T(8,128)} custom-call(bf16[3328,256]{1,0:T(8,128)(2,1)} %window.1, bf16[64,256]{1,0:T(8,128)(2,1)} %bitcast.1, f32[104,512]{1,0:T(8,128)} %panel.1, s32[2]{0:T(128)} %first.1), custom_call_target="tpu_custom_call" | custom-call | tf_op jit(solution)/shard_map/panel_update/pallas_call | solution.py:341
  53.6 1.6 %copy.6 = f32[104,512]{1,0:T(8,128)} copy(f32[104,512]{1,0:T(8,128)} %panel_update.1) | data formatting | bytes 425984

commit v4 on v3

--- a/solution.py
+++ b/solution.py
@@ -11,7 +11,8 @@
 ROWS = 104
 KC = 256
 GW = 64
-ROWS_A = 56
+PARTS = (56, 48)
+LEVELS = 32767.0
 POWERS = 7
 MESH = pl.DeviceIdType.MESH
 F32 = jnp.float32
@@ -23,15 +24,20 @@
     return hi, (v - hi.astype(F32)).astype(BF16)
 
 
+def coded(v):
+    step = jnp.maximum(jnp.max(jnp.abs(v), axis=0, keepdims=True) * (1.0 / LEVELS), 1e-37)
+    return jnp.round(v * (1.0 / step)).astype(jnp.int32).astype(jnp.int16), step
+
+
 def times_transposed(a, bt):
     return lax.dot_general(a, bt, (((1,), (1,)), ((), ())), preferred_element_type=F32)
 
 
 def kernel(
-    window, upper, panel, first, out,
-    ut, thr, pown, abuf, mbuf, msend, mrecv, ppan, piece, spread,
-    psend, precv, nsend, nrecv,
-    loc, sent, uy_r, th_r, ux_r, uc_r, a_r, m_r, pan_r, mz_r, xs_r, zs_r, ys_r, cs_r, ps_r, ns_r,
+    window, upper, panel, first_block, out,
+    first, ut, thr, pown, abuf, mbuf, msend, mrecv, ppan, piece, spread,
+    sums, codes, steps,
+    loc, sent, uy_r, th_r, ux_r, uc_r, a_r, m_r, pan_r, mz_r, xs_r, zs_r, ys_r, cs_r, ring_r,
 ):
     gr, gc = lax.axis_index("gr"), lax.axis_index("gc")
     x, c = gr // NC, gr % NC
@@ -60,6 +66,9 @@
 
     def arrived(like, sem):
         pltpu.make_async_copy(like, like, sem).wait()
+
+    first_own = pltpu.make_async_copy(first_block, first, loc.at[2])
+    first_own.start()
 
     barrier = pltpu.get_barrier_semaphore()
     for d in range(1, NY):
@@ -84,6 +93,7 @@
         return pl.ds(((y + d) % NY) * KC, KC)
 
     lane = lax.broadcasted_iota(jnp.int32, (8, KC), 1)
+    first_own.wait()
     thr[:, pl.ds(y * KC, KC)] = jnp.where(lane < BLK, first[0], first[1]) * BLK
     uy = [remote(upper, ut.at[group(0), cols(0)], sent.at[0], uy_r.at[d - 1], at_y(d)) for d in range(1, NY)]
     th = [
@@ -191,31 +201,38 @@
         arrived(abuf.at[i], a_r.at[i])
         return product(abuf[i], gr * (ROWS * NY * NZ) + (((z + order[i]) % NZ) * NY + y) * ROWS)
 
-    parts = (pl.ds(0, ROWS_A), pl.ds(ROWS_A, ROWS - ROWS_A))
-
-    def ring(send, recv, r, step):
+    parts = (pl.ds(0, PARTS[0]), pl.ds(PARTS[0], PARTS[1]))
+    PLUS, MINUS = 0, 1
+    hops = (at_z(1), at_z(NZ - 1))
+
+    def message(way, k, h):
+        at = 16 * way + 2 * k + h
+        rows = pl.ds(0, PARTS[h])
         return [
-            [remote(send.at[k, part, :], recv.at[k, part, :], sent.at[8], r.at[k, h], at_z(step)) for h, part in enumerate(parts)]
-            for k in range(4)
+            remote(codes.at[at, rows, :], codes.at[at + 8, rows, :], sent.at[8], ring_r.at[way, k, h], hops[way]),
+            remote(steps.at[at], steps.at[at + 8], sent.at[13], ring_r.at[way, k, h], hops[way]),
         ]
 
-    plus, minus = ring(psend, precv, ps_r, 1), ring(nsend, nrecv, ns_r, NZ - 1)
+    def send_on(way, k, h, v):
+        at = 16 * way + 2 * k + h
+        codes[at, pl.ds(0, PARTS[h]), :], steps[at] = coded(v)
+        for copy in message(way, k, h):
+            copy.start()
+
+    def came(way, k, h):
+        at = 16 * way + 2 * k + h + 8
+        arrived(steps.at[pl.ds(0, PARTS[h] // 2 + 1)], ring_r.at[way, k, h])
+        return codes[at, pl.ds(0, PARTS[h]), :].astype(jnp.int32).astype(F32) * steps[at]
 
     def forward(k, h):
-        plus[k - 1][h].wait_recv()
-        psend[k, parts[h], :] += precv[k - 1, parts[h], :]
-        plus[k][h].start()
-        minus[k - 1][1 - h].wait_recv()
-        nsend[k, parts[1 - h], :] += nrecv[k - 1, parts[1 - h], :]
-        minus[k][1 - h].start()
+        send_on(PLUS, k, h, sums[2 * k - 1, parts[h], :] + came(PLUS, k - 1, h))
+        send_on(MINUS, k, 1 - h, sums[2 * k, parts[1 - h], :] + came(MINUS, k - 1, 1 - h))
 
     update = chunk(0)
-    psend[0, parts[0], :] = update[:ROWS_A]
-    plus[0][0].start()
-    nsend[0, parts[1], :] = update[ROWS_A:]
-    minus[0][1].start()
-    psend[1] = chunk(1)
-    plus[1][1].start()
+    send_on(PLUS, 0, 0, update[: PARTS[0]])
+    send_on(MINUS, 0, 1, update[PARTS[0] :])
+    sums[1] = chunk(1)
+    send_on(PLUS, 1, 1, sums[1, parts[1], :])
     spread_x = [
         remote(piece.at[(d % NC)], spread.at[y, z, d % NC], sent.at[9], xs_r, (d, gc))
         for d in range(1, NX * NC)
@@ -253,11 +270,11 @@
             copy.start()
         spread_own()
 
-    nsend[1] = chunk(2)
-    minus[1][0].start()
+    sums[2] = chunk(2)
+    send_on(MINUS, 1, 0, sums[2, parts[0], :])
     forward(1, 0)
-    psend[2] = chunk(3)
-    nsend[2] = chunk(4)
+    sums[3] = chunk(3)
+    sums[4] = chunk(4)
     forward(2, 1)
 
     forward(2, 0)
@@ -268,8 +285,8 @@
         spread_own()
 
 
-    psend[3] = chunk(5)
-    nsend[3] = chunk(6)
+    sums[5] = chunk(5)
+    sums[6] = chunk(6)
     forward(3, 1)
     forward(3, 0)
 
@@ -283,12 +300,12 @@
     ]
     spread_c[0].start()
 
-    update = chunk(7)
+    sums[0] = chunk(7)
     panel_own.wait()
     for h in (1, 0):
-        plus[3][h].wait_recv()
-        minus[3][1 - h].wait_recv()
-    schur = pown[...] - (update + precv[3] + nrecv[3])
+        sums[0, parts[h], :] += came(PLUS, 3, h)
+        sums[0, parts[1 - h], :] += came(MINUS, 3, 1 - h)
+    schur = pown[...] - sums[0]
 
     for d in (1, 3, 2):
         arrived(spread.at[0, :, 0], ys_r.at[d - 1])
@@ -314,7 +331,8 @@
     arrived(ut.at[pl.ds(0, 3 * GW), :], sent.at[2])
     arrived(ut.at[pl.ds(0, PW // NC), :], sent.at[3])
     arrived(abuf.at[:, :, pl.ds(0, (NY - 1) * KC)], sent.at[5])
-    arrived(abuf.at[:, :, pl.ds(0, 7 * BLK)], sent.at[8])
+    arrived(codes.at[pl.ds(0, 13)], sent.at[8])
+    arrived(steps.at[pl.ds(0, 14)], sent.at[13])
     arrived(spread.at[0, pl.ds(0, NZ - 1), 0], sent.at[10])
     arrived(spread.at[pl.ds(0, NY - 1), :, 0], sent.at[11])
     arrived(spread.at[:, :, 0], sent.at[12])
@@ -341,9 +359,10 @@
     return pl.pallas_call(
         kernel,
         out_shape=jax.ShapeDtypeStruct((ROWS, PW), F32),
-        in_specs=[*[pl.BlockSpec(memory_space=pl.ANY)] * 3, pl.BlockSpec(memory_space=pltpu.SMEM)],
+        in_specs=[pl.BlockSpec(memory_space=pltpu.HBM)] * 4,
         out_specs=spec,
         scratch_shapes=[
+            pltpu.SMEM((2,), jnp.int32),
             vmem((PW, NY * KC), BF16),
             vmem((8, NY * KC), jnp.int32),
             vmem((ROWS, PW), F32),
@@ -354,16 +373,18 @@
             vmem((2, 8, PW), F32),
             vmem((2, 8, PW), F32),
             vmem((NY, NZ, NC, 8, PW), F32),
-            *[vmem((4, ROWS, PW), F32) for _ in range(4)],
-            dma((2,)), dma((13,)),
+            vmem((7, ROWS, PW), F32),
+            vmem((32, PARTS[0], PW), jnp.int16),
+            vmem((32, 1, PW), F32),
+            dma((3,)), dma((14,)),
             dma((NY - 1,)), dma, dma((NX - 1,)), dma, dma((NZ,)), dma, dma, dma, dma,
-            dma((NZ - 1,)), dma((NY - 1,)), dma, dma((4, 2)), dma((4, 2)),
+            dma((NZ - 1,)), dma((NY - 1,)), dma, dma((2, 4, 2)),
         ],
         compiler_params=pltpu.CompilerParams(
-            collective_id=0, has_side_effects=True, vmem_limit_bytes=63 * 1024 * 1024
+            collective_id=0, has_side_effects=True, vmem_limit_bytes=40 * 1024 * 1024
         ),
         name="panel_update",
-    )(window, upper.T, panel, first)
+    )(*[pltpu.with_memory_space_constraint(v, pltpu.HBM) for v in (window, upper.T, panel, first)])
 
 
 def solution(mesh):

time: 55.3 us -> 49.3 us (0.89)
  Pallas kernels: 53.6 us -> 48.6 us
  local copies, waits for them, and re-layouts: 1.63 us -> 0.69 us
    pallas_call x1, Pallas kernels: 53.6 us -> 48.6 us  [body(): pl.pallas_call(kernel, out_shape=jax.ShapeDtypeStruct((ROWS, PW), F32), i...]
    unnamed x1, local copies, waits for them, and re-layouts: 1.63 us -> 0.69 us
where the time goes in v4:
time: 49.3 us
  Pallas kernels  48.6 us (99%)
  local copies, waits for them, and re-layouts  0.69 us (1%)
    pallas_call x1, Pallas kernels, body(): pl.pallas_call(kernel, out_shape=jax.ShapeDtypeStruct((ROWS, PW), F32), i...  48.6 us

profile of v4, /device:TPU:1, one launch (start us, length us, event | category | flops | bytes accessed | tf_op | source)
XLA Modules:
  0.0 49.3 jit_solution(4595955212707678147)
XLA Ops:
  0.0 48.6 %panel_update.1 = f32[104,512]{1,0:T(8,128)S(1)} custom-call(bf16[3328,256]{1,0:T(8,128)(2,1)} %window.1, bf16[64,256]{1,0:T(8,128)(2,1)} %bitcast.1, f32[104,512]{1,0:T(8,128)} %panel.1, s32[2]{0:T(128)} %first_block.1), custom_call_target="tpu_custom_call" | custom-call | tf_op jit(solution)/shard_map/panel_update/pallas_call | solution.py:359
  48.6 0.7 %copy.6 = f32[104,512]{1,0:T(8,128)} copy(f32[104,512]{1,0:T(8,128)S(1)} %panel_update.1) | data formatting | bytes 425984

commit v5 on v4

--- a/solution.py
+++ b/solution.py
@@ -35,9 +35,9 @@
 
 def kernel(
     window, upper, panel, first_block, out,
-    first, ut, thr, pown, abuf, mbuf, msend, mrecv, ppan, piece, spread,
+    first, ut, thr, pown, abuf, mbuf, msend, mcodes, msteps, ppan, piece, spread,
     sums, codes, steps,
-    loc, sent, uy_r, th_r, ux_r, uc_r, a_r, m_r, pan_r, mz_r, xs_r, zs_r, ys_r, cs_r, ring_r,
+    loc, sent, uy_r, th_r, ux_r, uc_r, a_r, m_r, pan_r, mz_r, mzs_r, xs_r, zs_r, ys_r, cs_r, ring_r,
 ):
     gr, gc = lax.axis_index("gr"), lax.axis_index("gc")
     x, c = gr // NC, gr % NC
@@ -186,7 +186,10 @@
         return times_transposed(kept, ut[...])
 
     mz = [
-        remote(msend.at[pl.ds(((z + d) % NZ) * 16, 16), :], mrecv.at[d - 1], sent.at[7], mz_r, at_z(d))
+        [
+            remote(mcodes.at[(z + d) % NZ], mcodes.at[NZ + d - 1], sent.at[7], mz_r, at_z(d)),
+            remote(msteps.at[(z + d) % NZ], msteps.at[NZ + d - 1], sent.at[14], mzs_r, at_z(d)),
+        ]
         for d in range(1, NZ)
     ]
 
@@ -194,8 +197,11 @@
     def _():
         arrived(mbuf, m_r)
         msend[...] = product(mbuf[...], y * BLK)
-        for copy in mz:
-            copy.start()
+        for k in range(NZ):
+            mcodes[k], msteps[k] = coded(msend[pl.ds(16 * k, 16), :])
+        for d in (4, 3, 5, 2, 6, 1, 7):
+            for copy in mz[d - 1]:
+                copy.start()
 
     def chunk(i):
         arrived(abuf.at[i], a_r.at[i])
@@ -231,8 +237,6 @@
     update = chunk(0)
     send_on(PLUS, 0, 0, update[: PARTS[0]])
     send_on(MINUS, 0, 1, update[PARTS[0] :])
-    sums[1] = chunk(1)
-    send_on(PLUS, 1, 1, sums[1, parts[1], :])
     spread_x = [
         remote(piece.at[(d % NC)], spread.at[y, z, d % NC], sent.at[9], xs_r, (d, gc))
         for d in range(1, NX * NC)
@@ -251,25 +255,28 @@
     ]
 
     def spread_own():
-        for d in (4, 3, 5, 2, 6, 1, 7):
+        for d in (1, 7, 2, 6, 3, 5, 4):
             spread_z[d - 1].start()
         for d in (1, 3, 2):
             spread_y[d - 1][0].start()
 
     @pl.when(pivot_plane)
     def _():
-        arrived(mrecv, mz_r)
+        arrived(mcodes.at[pl.ds(0, NZ - 1)], mz_r)
+        arrived(msteps.at[pl.ds(0, NZ - 1)], mzs_r)
         arrived(ppan, pan_r)
         total = msend[pl.ds(z * 16, 16), :]
         for d in range(1, NZ):
-            total = total + mrecv[d - 1]
+            total = total + mcodes[NZ + d - 1].astype(jnp.int32).astype(F32) * msteps[NZ + d - 1]
         for s in range(2):
             piece[s] = ppan[s] - total[8 * s : 8 * s + 8]
         spread[y, z, 0] = piece[0]
-        for copy in spread_x:
-            copy.start()
+        for d in (4, 5, 2, 3, 6, 7, 1):
+            spread_x[d - 1].start()
         spread_own()
 
+    sums[1] = chunk(1)
+    send_on(PLUS, 1, 1, sums[1, parts[1], :])
     sums[2] = chunk(2)
     send_on(MINUS, 1, 0, sums[2, parts[0], :])
     forward(1, 0)
@@ -285,15 +292,20 @@
         spread_own()
 
 
+    def came_along_z(which):
+        for j in which:
+            spread_z[j - 1].wait_recv()
+            for d in (1, 3, 2):
+                spread_y[d - 1][j].start()
+
+    came_along_z((1, 7))
     sums[5] = chunk(5)
+    came_along_z((2, 6))
     sums[6] = chunk(6)
     forward(3, 1)
     forward(3, 0)
 
-    for j in (1, 7, 2, 6, 3, 5, 4):
-        spread_z[j - 1].wait_recv()
-        for d in (1, 3, 2):
-            spread_y[d - 1][j].start()
+    came_along_z((3, 5, 4))
     spread_c = [
         remote(spread.at[(y + NY - d) % NY, :, c], spread.at[(y + NY - d) % NY, :, c], sent.at[12], cs_r, other_core)
         for d in range(NY)
@@ -340,7 +352,8 @@
     @pl.when(pivot_plane)
     def _():
         arrived(mbuf.at[:, pl.ds(0, (NY - 1) * KC)], sent.at[4])
-        arrived(mrecv, sent.at[7])
+        arrived(mcodes.at[pl.ds(0, NZ - 1)], sent.at[7])
+        arrived(msteps.at[pl.ds(0, NZ - 1)], sent.at[14])
         arrived(spread.at[0, pl.ds(0, NZ - 1), 0], sent.at[9])
 
     @pl.when(jnp.logical_and(gr == 0, gc < 4))
@@ -369,15 +382,16 @@
             vmem((NZ, ROWS, NY * KC), BF16),
             vmem((BLK, NY * KC), BF16),
             vmem((BLK, PW), F32),
-            vmem((NZ - 1, 16, PW), F32),
+            vmem((2 * NZ - 1, 16, PW), jnp.int16),
+            vmem((2 * NZ - 1, 1, PW), F32),
             vmem((2, 8, PW), F32),
             vmem((2, 8, PW), F32),
             vmem((NY, NZ, NC, 8, PW), F32),
             vmem((7, ROWS, PW), F32),
             vmem((32, PARTS[0], PW), jnp.int16),
             vmem((32, 1, PW), F32),
-            dma((3,)), dma((14,)),
-            dma((NY - 1,)), dma, dma((NX - 1,)), dma, dma((NZ,)), dma, dma, dma, dma,
+            dma((3,)), dma((15,)),
+            dma((NY - 1,)), dma, dma((NX - 1,)), dma, dma((NZ,)), dma, dma, dma, dma, dma,
             dma((NZ - 1,)), dma((NY - 1,)), dma, dma((2, 4, 2)),
         ],
         compiler_params=pltpu.CompilerParams(

time: 49.3 us -> 46.7 us (0.947)
  Pallas kernels: 48.6 us -> 45.9 us
    pallas_call x1, Pallas kernels: 48.6 us -> 45.9 us  [body(): pl.pallas_call(kernel, out_shape=jax.ShapeDtypeStruct((ROWS, PW), F32), i...]
where the time goes in v5:
time: 46.7 us; the launch traced here: 46.6 us
  Pallas kernels  45.9 us (98%)
  local copies, waits for them, and re-layouts  0.69 us (1%)
    pallas_call x1, Pallas kernels, body(): pl.pallas_call(kernel, out_shape=jax.ShapeDtypeStruct((ROWS, PW), F32), i...  45.9 us

profile of v5, /device:TPU:1, one launch (start us, length us, event | category | flops | bytes accessed | tf_op | source)
XLA Modules:
  0.0 46.6 jit_solution(358240324989103313)
XLA Ops:
  0.0 45.9 %panel_update.1 = f32[104,512]{1,0:T(8,128)S(1)} custom-call(bf16[3328,256]{1,0:T(8,128)(2,1)} %window.1, bf16[64,256]{1,0:T(8,128)(2,1)} %bitcast.1, f32[104,512]{1,0:T(8,128)} %panel.1, s32[2]{0:T(128)} %first_block.1), custom_call_target="tpu_custom_call" | custom-call | tf_op jit(solution)/shard_map/panel_update/pallas_call | solution.py:372
  45.9 0.7 %copy.6 = f32[104,512]{1,0:T(8,128)} copy(f32[104,512]{1,0:T(8,128)S(1)} %panel_update.1) | data formatting | bytes 425984

commit v6 on v5

--- a/solution.py
+++ b/solution.py
@@ -277,14 +277,23 @@
 
     sums[1] = chunk(1)
     send_on(PLUS, 1, 1, sums[1, parts[1], :])
+    other_planes = jnp.logical_not(pivot_plane)
+
+    def came_along_z(which, where):
+        @pl.when(where)
+        def _():
+            for j in which:
+                spread_z[j - 1].wait_recv()
+                for d in (1, 3, 2):
+                    spread_y[d - 1][j].start()
+
     sums[2] = chunk(2)
     send_on(MINUS, 1, 0, sums[2, parts[0], :])
     forward(1, 0)
     sums[3] = chunk(3)
     sums[4] = chunk(4)
+    came_along_z((1, 7, 2, 6), pivot_plane)
     forward(2, 1)
-
-    forward(2, 0)
 
     @pl.when(jnp.logical_not(pivot_plane))
     def _():
@@ -292,25 +301,31 @@
         spread_own()
 
 
-    def came_along_z(which):
-        for j in which:
-            spread_z[j - 1].wait_recv()
-            for d in (1, 3, 2):
-                spread_y[d - 1][j].start()
-
-    came_along_z((1, 7))
+    came_along_z((3, 5, 4), pivot_plane)
+    forward(2, 0)
+
+    came_along_z((1, 7), other_planes)
     sums[5] = chunk(5)
-    came_along_z((2, 6))
+    came_along_z((2, 6), other_planes)
     sums[6] = chunk(6)
     forward(3, 1)
     forward(3, 0)
 
-    came_along_z((3, 5, 4))
+    came_along_z((3, 5, 4), other_planes)
     spread_c = [
         remote(spread.at[(y + NY - d) % NY, :, c], spread.at[(y + NY - d) % NY, :, c], sent.at[12], cs_r, other_core)
         for d in range(NY)
     ]
     spread_c[0].start()
+
+    def came_along_y(where):
+        @pl.when(where)
+        def _():
+            for d in (1, 3, 2):
+                arrived(spread.at[0, :, 0], ys_r.at[d - 1])
+                spread_c[d].start()
+
+    came_along_y(gr >= 0)
 
     sums[0] = chunk(7)
     panel_own.wait()
@@ -319,15 +334,17 @@
         sums[0, parts[1 - h], :] += came(MINUS, 3, 1 - h)
     schur = pown[...] - sums[0]
 
-    for d in (1, 3, 2):
-        arrived(spread.at[0, :, 0], ys_r.at[d - 1])
-        spread_c[d].start()
     arrived(spread.at[:, :, 0], cs_r)
 
     pivot = spread[...].reshape(PW, PW)
+    same = lax.broadcasted_iota(jnp.int32, (BLK, BLK), 0) == lax.broadcasted_iota(jnp.int32, (BLK, BLK), 1)
+    diagonal = [jnp.where(same, pivot[k : k + BLK, k : k + BLK], 0.0) for k in range(0, PW, BLK)]
+    diagonal = (diagonal[0] + diagonal[1]) + (diagonal[2] + diagonal[3])
+    scale = jnp.sum(jnp.sum(diagonal, axis=0, keepdims=True), axis=1, keepdims=True) / PW
+    near = jnp.where(jnp.abs(scale) > 1.0, 2.0**-64, 2.0**64)
+    inverse_scale = 1.0 / (scale * near)
     same = lax.broadcasted_iota(jnp.int32, (PW, PW), 0) == lax.broadcasted_iota(jnp.int32, (PW, PW), 1)
-    scale = jnp.sum(jnp.sum(jnp.where(same, pivot, 0.0), axis=0, keepdims=True), axis=1, keepdims=True) / PW
-    rest_hi, rest_lo = split(jnp.where(same, 1.0, 0.0) - pivot / scale)
+    rest_hi, rest_lo = split(jnp.where(same, 1.0, 0.0) - (pivot * near) * inverse_scale)
     row_ids = (gr * NY * NZ + gc) * ROWS + lax.broadcasted_iota(jnp.int32, (ROWS, PW), 0)
     unit = jnp.where(row_ids == lax.broadcasted_iota(jnp.int32, (ROWS, PW), 1), 1.0, 0.0)
     left = jnp.where(row_ids < PW, unit, schur / scale)

time: 46.7 us -> 44.5 us (0.953)
  the two profiles are of different devices: /device:TPU:1 before, /device:TPU:3 now
where the time goes in v6:
time: 44.5 us
  Pallas kernels  43.8 us (98%)
  local copies, waits for them, and re-layouts  0.69 us (2%)
    pallas_call x1, Pallas kernels, body(): pl.pallas_call(kernel, out_shape=jax.ShapeDtypeStruct((ROWS, PW), F32), i...  43.8 us

profile of v6, /device:TPU:3, one launch (start us, length us, event | category | flops | bytes accessed | tf_op | source)
XLA Modules:
  0.0 44.5 jit_solution(16657935465912954156)
XLA Ops:
  0.0 43.8 %panel_update.1 = f32[104,512]{1,0:T(8,128)S(1)} custom-call(bf16[3328,256]{1,0:T(8,128)(2,1)} %window.1, bf16[64,256]{1,0:T(8,128)(2,1)} %bitcast.1, f32[104,512]{1,0:T(8,128)} %panel.1, s32[2]{0:T(128)} %first_block.1), custom_call_target="tpu_custom_call" | custom-call | tf_op jit(solution)/shard_map/panel_update/pallas_call | solution.py:389
  43.8 0.7 %copy.6 = f32[104,512]{1,0:T(8,128)} copy(f32[104,512]{1,0:T(8,128)S(1)} %panel_update.1) | data formatting | bytes 425984

commit v7 on v6

--- a/solution.py
+++ b/solution.py
@@ -84,30 +84,33 @@
         def _():
             pl.semaphore_signal(barrier, inc=1, device_id=(0, owner), device_id_type=MESH)
 
-    pl.semaphore_wait(barrier, 17 + jnp.where(panel_source, 11 + gc // 4, 0))
-
     def group(d):
         return pl.ds((((x + d) % NX) * NC + c) * GW, GW)
 
     def cols(d):
         return pl.ds(((y + d) % NY) * KC, KC)
 
+    upper_own = pltpu.make_async_copy(upper, ut.at[group(0), cols(0)], loc.at[0])
+    upper_own.start()
     lane = lax.broadcasted_iota(jnp.int32, (8, KC), 1)
     first_own.wait()
     thr[:, pl.ds(y * KC, KC)] = jnp.where(lane < BLK, first[0], first[1]) * BLK
-    uy = [remote(upper, ut.at[group(0), cols(0)], sent.at[0], uy_r.at[d - 1], at_y(d)) for d in range(1, NY)]
+    upper_own.wait()
+
+    pl.semaphore_wait(barrier, 17 + jnp.where(panel_source, 11 + gc // 4, 0))
+
+    uy = [remote(ut.at[group(0), cols(0)], ut.at[group(0), cols(0)], sent.at[0], uy_r.at[d - 1], at_y(d)) for d in range(1, NY)]
     th = [
         remote(thr.at[:, cols(0)], thr.at[:, cols(0)], sent.at[1], th_r, at_y(d)) for d in range(1, NY)
     ]
     ux = [
         [
-            remote(ut.at[group(0), cols(-j)] if j else upper, ut.at[group(0), cols(-j)],
+            remote(ut.at[group(0), cols(-j)], ut.at[group(0), cols(-j)],
                    sent.at[2], ux_r.at[d - 1], at_x(d))
             for j in range(NY)
         ]
         for d in range(1, NX)
     ]
-    upper_own = pltpu.make_async_copy(upper, ut.at[group(0), cols(0)], loc.at[0])
     panel_own = pltpu.make_async_copy(panel, pown, loc.at[1])
     for d in (1, 3, 2):
         uy[d - 1].start()
@@ -115,7 +118,6 @@
         ux[d - 1][0].start()
     for copy in th:
         copy.start()
-    upper_own.start()
 
     mini = [
         remote(window.at[pl.ds(((y + d) % NY) * BLK, BLK), :], mbuf.at[:, pl.ds(y * KC, KC)],
@@ -172,7 +174,6 @@
         for d in (1, 3, 2):
             ux[d - 1][j].start()
     uc = [remote(ut.at[group(-d), :], ut.at[group(-d), :], sent.at[3], uc_r, other_core) for d in range(NX)]
-    upper_own.wait()
     uc[0].start()
     for d in (1, 3, 2):
         arrived(ut.at[group(-d), :], ux_r.at[d - 1])

time: 44.5 us -> 44.4 us (level)
  no operation moved by 1% of the time
where the time goes in v7:
time: 44.4 us; the launch traced here: 44.2 us
  Pallas kernels  43.5 us (98%)
  local copies, waits for them, and re-layouts  0.69 us (2%)
    pallas_call x1, Pallas kernels, body(): pl.pallas_call(kernel, out_shape=jax.ShapeDtypeStruct((ROWS, PW), F32), i...  43.5 us

profile of v7, /device:TPU:3, one launch (start us, length us, event | category | flops | bytes accessed | tf_op | source)
XLA Modules:
  0.0 44.2 jit_solution(6963337918224772040)
XLA Ops:
  0.0 43.5 %panel_update.1 = f32[104,512]{1,0:T(8,128)S(1)} custom-call(bf16[3328,256]{1,0:T(8,128)(2,1)} %window.1, bf16[64,256]{1,0:T(8,128)(2,1)} %bitcast.1, f32[104,512]{1,0:T(8,128)} %panel.1, s32[2]{0:T(128)} %first_block.1), custom_call_target="tpu_custom_call" | custom-call | tf_op jit(solution)/shard_map/panel_update/pallas_call | solution.py:390
  43.5 0.7 %copy.6 = f32[104,512]{1,0:T(8,128)} copy(f32[104,512]{1,0:T(8,128)S(1)} %panel_update.1) | data formatting | bytes 425984

commit v8 on v7

--- a/solution.py
+++ b/solution.py
@@ -147,7 +147,7 @@
         own_rows.append(
             pltpu.make_async_copy(window.at[rows_of(i, y), :], abuf.at[i, :, pl.ds(y * KC, KC)], a_r.at[i])
         )
-        for copy in exchange[i]:
+        for copy in exchange[i] if i < NZ - 1 else []:
             copy.start()
         own_rows[i].start()
 
@@ -260,6 +260,8 @@
             spread_z[d - 1].start()
         for d in (1, 3, 2):
             spread_y[d - 1][0].start()
+        for copy in exchange[NZ - 1]:
+            copy.start()
 
     @pl.when(pivot_plane)
     def _():

time: 44.4 us -> 44.4 us (level)
  no operation moved by 1% of the time
where the time goes in v8:
time: 44.4 us; the launch traced here: 44.2 us
  Pallas kernels  43.5 us (98%)
  local copies, waits for them, and re-layouts  0.69 us (2%)
    pallas_call x1, Pallas kernels, body(): pl.pallas_call(kernel, out_shape=jax.ShapeDtypeStruct((ROWS, PW), F32), i...  43.5 us

profile of v8, /device:TPU:3, one launch (start us, length us, event | category | flops | bytes accessed | tf_op | source)
XLA Modules:
  0.0 44.2 jit_solution(9625511570622208752)
XLA Ops:
  0.0 43.5 %panel_update.1 = f32[104,512]{1,0:T(8,128)S(1)} custom-call(bf16[3328,256]{1,0:T(8,128)(2,1)} %window.1, bf16[64,256]{1,0:T(8,128)(2,1)} %bitcast.1, f32[104,512]{1,0:T(8,128)} %panel.1, s32[2]{0:T(128)} %first_block.1), custom_call_target="tpu_custom_call" | custom-call | tf_op jit(solution)/shard_map/panel_update/pallas_call | solution.py:392
  43.5 0.7 %copy.6 = f32[104,512]{1,0:T(8,128)} copy(f32[104,512]{1,0:T(8,128)S(1)} %panel_update.1) | data formatting | bytes 425984
